TPU v7x, 128 devices: a whole 4x4x4 slice. The times are simulated.
128 devices in a mesh: tile: 32 (over z_hi, x, y), blk: 4 (over z_lo, core).
Axes of the slice: x: 4, y: 4, z: 4 (z_hi: 2, z_lo: 2; z = z_hi * 2 + z_lo), core: 2. Of those that a mesh axis runs over, the one named last changes fastest.
Arguments:
- image_tokens: bfloat16 [16, 1024, 1536], P(None, 'tile', 'blk'), may hold values from -10 to 10
- text_tokens: bfloat16 [16, 160, 1536], P(None, 'tile', 'blk'), may hold values from -10 to 10
- step_index: int32 [16], replicated, may hold values from 0 to 27
- text_length: int32 [16], replicated, may hold values from 1 to 160, as said below
- image_table: bfloat16 [28, 6, 1536], replicated, may hold values from -3 to 3
- text_table: bfloat16 [28, 3, 1536], replicated, may hold values from -3 to 3
- qkv_image: bfloat16 [1536, 3, 1536], P(None, None, 'blk'), may hold values from -0.15625 to 0.15625
- qkv_text: bfloat16 [1536, 3, 1536], P(None, None, 'blk'), may hold values from -0.15625 to 0.15625
- attn_out_image: bfloat16 [1536, 1536], P('blk'), may hold values from -0.15625 to 0.15625
- attn_out_text: bfloat16 [1536, 1536], P('blk'), may hold values from -0.15625 to 0.15625
- query_gain_image: float32 [64], replicated, may hold values from 1 to 12
- key_gain_image: float32 [64], replicated, may hold values from 1 to 12
- query_gain_text: float32 [64], replicated, may hold values from 1 to 12
- key_gain_text: float32 [64], replicated, may hold values from 1 to 12
- up_weight: bfloat16 [1536, 6144], P(None, 'blk'), may hold values from -0.15625 to 0.15625
- down_weight: bfloat16 [6144, 1536], P('blk'), may hold values from -0.078125 to 0.078125
Outputs:
- image_out: bfloat16 [16, 1024, 1536], P(None, 'tile', 'blk')
- text_out: bfloat16 [16, 160, 1536], P(None, 'tile', 'blk')
Inputs may be any that keep to these rules, and one draw needn't show every extreme that they name: `text_length`: some request has all 160 slots valid.
All inputs are finite; a program needn't handle non-finite values.
Results may differ from a plain program's by a relative error of at most 0.015.
The roundings to bfloat16 on the way count: a program that leaves them out, or rounds other values in their place, can miss the bound.
Values may be sent and summed in bfloat16 or wider, within the bound.
No kernel may reach another device: no remote copies, remote signals or barrier semaphores. Data moves between devices by JAX's collectives and lax.ppermute only.
A program may use at most 192 MiB of HBM per device.

v0:
```python
import jax
import jax.numpy as jnp
from jax import lax
from jax.sharding import PartitionSpec as P

HEAD_DIM = 64
masked_score = -1e30


def layer_norm(values):
    centre = jnp.mean(values, axis=-1, keepdims=True)
    spread = jnp.mean(jnp.square(values - centre), axis=-1, keepdims=True)
    return (values - centre) * lax.rsqrt(spread + 1e-06)


def modulate(normed, shift_rows, scale_rows):
    return (normed * (1.0 + scale_rows[:, None, :]) + shift_rows[:, None, :]).astype(jnp.bfloat16)


def lookup(table_rows, step_index):
    picker = (step_index[:, None] == jnp.arange(table_rows.shape[0])[None, :]).astype(
        table_rows.dtype
    )
    return jnp.einsum("rs,skd->rkd", picker, table_rows, preferred_element_type=jnp.float32)


def head_norm(values, gain_vector):
    inverse_rms = lax.rsqrt(jnp.mean(jnp.square(values), axis=-1, keepdims=True) + 1e-06)
    return (values * inverse_rms * gain_vector).astype(jnp.bfloat16)


def project_heads(activations, weight, gain_query, gain_key):
    projected = jnp.einsum("rsd,dke->rske", activations, weight, preferred_element_type=jnp.float32)
    split_shape = projected.shape[:2] + (projected.shape[3] // HEAD_DIM, HEAD_DIM)
    query_heads = head_norm(projected[:, :, 0].reshape(split_shape), gain_query)
    key_heads = head_norm(projected[:, :, 1].reshape(split_shape), gain_key)
    value_heads = projected[:, :, 2].reshape(split_shape).astype(jnp.bfloat16)
    return (query_heads, key_heads, value_heads)


def per_device(
    image_tokens,
    text_tokens,
    step_index,
    text_length,
    image_table,
    text_table,
    qkv_image,
    qkv_text,
    attn_out_image,
    attn_out_text,
    query_gain_image,
    key_gain_image,
    query_gain_text,
    key_gain_text,
    up_weight,
    down_weight,
):
    requests = image_tokens.shape[0]
    image_rows = image_tokens.shape[1]
    text_rows = text_tokens.shape[1]
    joint_rows = image_rows + text_rows
    part_width = image_tokens.shape[2]
    column_start = lax.axis_index("blk") * part_width
    scale_factor = HEAD_DIM ** (-0.5)
    image_mods = lookup(image_table, step_index)
    text_mods = lookup(text_table, step_index)
    image_local = lax.dynamic_slice_in_dim(image_mods, column_start, part_width, 2)
    text_local = lax.dynamic_slice_in_dim(text_mods, column_start, part_width, 2)
    image_float = image_tokens.astype(jnp.float32)
    text_float = text_tokens.astype(jnp.float32)
    image_whole, text_whole = (
        lax.all_gather(image_tokens, "blk", axis=2, tiled=True),
        lax.all_gather(text_tokens, "blk", axis=2, tiled=True),
    )
    image_acts = modulate(
        layer_norm(image_whole.astype(jnp.float32)), image_mods[:, 0], image_mods[:, 1]
    )
    text_acts = modulate(
        layer_norm(text_whole.astype(jnp.float32)), text_mods[:, 0], text_mods[:, 1]
    )
    image_q, image_k, image_v = project_heads(
        image_acts, qkv_image, query_gain_image, key_gain_image
    )
    text_q, text_k, text_v = project_heads(text_acts, qkv_text, query_gain_text, key_gain_text)
    joint_q = jnp.concatenate([image_q, text_q], axis=1)
    joint_k = jnp.concatenate([image_k, text_k], axis=1)
    joint_v = jnp.concatenate([image_v, text_v], axis=1)
    head_count = joint_q.shape[2]
    key_value = jnp.stack(
        [
            joint_k.reshape(requests, joint_rows, part_width),
            joint_v.reshape(requests, joint_rows, part_width),
        ],
        axis=2,
    )
    shard_piece = lax.all_gather(key_value, "tile", axis=1, tiled=True)
    running_max = jnp.full((requests, head_count, joint_rows, 1), masked_score, jnp.float32)
    piece_rows = shard_piece.shape[1]
    position = jnp.arange(piece_rows, dtype=jnp.int32)
    offset = position % joint_rows
    text_slot = position // joint_rows * text_rows + offset - image_rows
    visible = (offset < image_rows)[None, :] | (text_slot[None, :] < text_length[:, None])
    piece_keys = shard_piece[:, :, 0].reshape(requests, piece_rows, head_count, HEAD_DIM)
    piece_values = shard_piece[:, :, 1].reshape(requests, piece_rows, head_count, HEAD_DIM)
    scores = (
        jnp.einsum("rqhe,rkhe->rhqk", joint_q, piece_keys, preferred_element_type=jnp.float32)
        * scale_factor
    )
    visible_mask = visible[:, None, None, :]
    new_max = jnp.maximum(
        running_max, jnp.max(jnp.where(visible_mask, scores, masked_score), axis=-1, keepdims=True)
    )
    weights = jnp.where(visible_mask, jnp.exp(scores - new_max), 0.0)
    running_sum = jnp.sum(weights, axis=-1, keepdims=True)
    running_out = jnp.einsum(
        "rhqk,rkhe->rhqe",
        weights.astype(jnp.bfloat16),
        piece_values,
        preferred_element_type=jnp.float32,
    )
    attended = (
        jnp.transpose(running_out / running_sum, (0, 2, 1, 3))
        .astype(jnp.bfloat16)
        .reshape(requests, joint_rows, part_width)
    )
    image_term = jnp.einsum(
        "rsd,de->rse", attended[:, :image_rows], attn_out_image, preferred_element_type=jnp.float32
    )
    text_term = jnp.einsum(
        "rsd,de->rse", attended[:, image_rows:], attn_out_text, preferred_element_type=jnp.float32
    )
    image_proj, text_proj = (
        lax.psum_scatter(
            image_term.astype(jnp.bfloat16), "blk", scatter_dimension=2, tiled=True
        ).astype(jnp.float32),
        lax.psum_scatter(
            text_term.astype(jnp.bfloat16), "blk", scatter_dimension=2, tiled=True
        ).astype(jnp.float32),
    )
    image_mid = (image_float + image_local[:, 2][:, None, :] * image_proj).astype(jnp.bfloat16)
    text_out = (text_float + text_local[:, 2][:, None, :] * text_proj).astype(jnp.bfloat16)
    middle_float = image_mid.astype(jnp.float32)
    middle_whole = lax.all_gather(image_mid, "blk", axis=2, tiled=True)
    mlp_input = modulate(
        layer_norm(middle_whole.astype(jnp.float32)), image_mods[:, 3], image_mods[:, 4]
    )
    hidden = jax.nn.gelu(
        jnp.einsum("rsd,df->rsf", mlp_input, up_weight, preferred_element_type=jnp.float32),
        approximate=True,
    ).astype(jnp.bfloat16)
    down_term = jnp.einsum("rsf,fd->rsd", hidden, down_weight, preferred_element_type=jnp.float32)
    down_sum = lax.psum_scatter(
        down_term.astype(jnp.bfloat16), "blk", scatter_dimension=2, tiled=True
    ).astype(jnp.float32)
    image_out = (middle_float + image_local[:, 5][:, None, :] * down_sum).astype(jnp.bfloat16)
    return (image_out, text_out)


def solution(mesh):
    in_specs = (
        P(None, "tile", "blk"),
        P(None, "tile", "blk"),
        P(),
        P(),
        P(),
        P(),
        P(None, None, "blk"),
        P(None, None, "blk"),
        P("blk", None),
        P("blk", None),
        P(),
        P(),
        P(),
        P(),
        P(None, "blk"),
        P("blk", None),
    )
    out_specs = (P(None, "tile", "blk"), P(None, "tile", "blk"))
    return jax.shard_map(
        per_device, mesh=mesh, in_specs=in_specs, out_specs=out_specs, check_vma=False
    )
```

profile of v0, /device:TPU:1, one launch (start us, length us, event | category | flops | bytes accessed | tf_op | source)
XLA Modules:
  0.0 523.8 jit_solution(4415324707470170074)
XLA Ops:
  9.7 7.6 %all_gather.13 = bf16[16,5,1536]{2,0,1:T(8,128)(2,1)S(1)} all-gather(bf16[16,5,384]{2,0,1:T(8,128)(2,1)} %param.17), channel_id=1, replica_groups=mesh['tile'=32,'blk'=4] {'blk'}, dimensions={2}, use_global_device_ids=true | all-gather | bytes 307200 | tf_op jit(solution)/shard_map/all_gather | solution.py:74
  19.6 2.8 fusion.16
  36.0 2.2 all-gather.4.cloned.1.call-done
  38.2 1.8 convert_reduce_fusion.1
  40.1 2.0 fusion.24
  42.1 2.4 fusion.18
  49.6 1.8 fusion.115
  55.6 230.7 %all-gather.6.cloned.1.call-done = bf16[16,1184,2,384]{3,0,2,1:T(8,128)(2,1)} async-done(((bf16[16,37,2,384]{3,0,2,1:T(8,128)(2,1)}), bf16[16,1184,2,384]{3,0,2,1:T(8,128)(2,1)}) %all-gather.6.cloned.1.call-update) | async-done | bytes 29098000 | tf_op jit(solution)/shard_map/all_gather | solution.py:97
  286.4 21.9 %fusion.114 = (bf16[16,1184,1,384]{3,0,2,1:T(8,128)(2,1)}, bf16[16,1184,1,384]{3,0,2,1:T(8,128)(2,1)}) fusion(bf16[16,1184,2,384]{3,0,2,1:T(8,128)(2,1)} %all-gather.6.cloned.1.call-done), kind=kLoop, calls=%fused_computation.149 | loop fusion | bytes 58195968 | tf_op jit(solution)/shard_map/slice | solution.py:104
  308.2 20.2 %copy.78 = bf16[16,1184,1,384]{1,3,0,2:T(8,128)(2,1)} copy(bf16[16,1184,1,384]{3,0,2,1:T(8,128)(2,1)} %get-tuple-element.2) | data formatting | bytes 29097984
  328.5 12.2 %select_reduce_fusion = (f32[16,6,37]{2,1,0:T(8,128)S(1)}, f32[16,6,37,1184]{3,2,1,0:T(8,128)}) fusion(pred[16,1184]{1,0:T(8,128)(4,1)S(1)} %compare_or_fusion, bf16[16,1184,6,64]{1,3,2,0:T(8,128)(2,1)} %bitcast.109, bf16[16,5,6,64]{3,1,2,0:T(8,128)(2,1)S(1)} %fusion.79, bf16[16,32,6,64]{3,1,2,0:T(8,128)(2,1)S(1)} %fusion.50), kind=kOutput, calls=%fused_computation.1 | convolution fusion | flops 551835136 | bytes 31859072 | tf_op jit(solution)/shard_map/rqhe,rkhe->rhqk/dot_general | solution.py:107
  340.7 20.2 %copy.79 = bf16[16,1184,1,384]{1,3,0,2:T(8,128)(2,1)} copy(bf16[16,1184,1,384]{3,0,2,1:T(8,128)(2,1)} %get-tuple-element.3) | data formatting | bytes 29097984
  360.9 9.8 %fusion = f32[16,6,37]{2,1,0:T(8,128)S(1)} fusion(f32[16,6,37,1184]{3,2,1,0:T(8,128)} %get-tuple-element.17, f32[16,6,37]{2,1,0:T(8,128)S(1)} %broadcast_maximum_fusion, pred[16,1184]{1,0:T(8,128)(4,1)S(1)} %compare_or_fusion), kind=kLoop, calls=%fused_computation.2 | loop fusion | flops 16818720 | bytes 16869632 | tf_op jit(solution)/shard_map/reduce_sum | solution.py:115
  370.7 13.1 %fusion.43 = bf16[16,37,6,64]{3,1,2,0:T(8,128)(2,1)S(1)} fusion(bf16[16,1184,6,64]{1,3,2,0:T(8,128)(2,1)} %bitcast.112, f32[16,6,37,1184]{3,2,1,0:T(8,128)} %get-tuple-element.17, f32[16,6,37]{2,1,0:T(8,128)S(1)} %broadcast_maximum_fusion, pred[16,1184]{1,0:T(8,128)(4,1)S(1)} %compare_or_fusion, f32[16,37,6]{1,2,0:T(8,128)S(1)} %bitcast.117), kind=kOutput, calls=%fused_computation.47 | convolution fusion | flops 555589632 | bytes 31873280 | tf_op jit(solution)/shard_map/rhqk,rkhe->rhqe/dot_general | solution.py:116
  385.0 2.3 convolution_convert_fusion
  387.2 6.6 %copy.72 = bf16[16,32,1536]{1,0,2:T(8,128)(2,1)} copy(bf16[16,32,1536]{2,1,0:T(8,128)(2,1)S(1)} %convolution_convert_fusion) | data formatting | bytes 3145728
  393.8 9.3 %reshape.168 = bf16[1536,512]{1,0:T(8,128)(2,1)} reshape(bf16[1536,16,32]{2,1,0:T(8,128)(2,1)} %bitcast.110) | data formatting | bytes 3145728
  404.8 20.8 %reduce-scatter.10.cloned.1.call-done = bf16[384,512]{1,0:T(8,128)(2,1)} async-done(((bf16[1536,512]{1,0:T(8,128)(2,1)}), bf16[384,512]{1,0:T(8,128)(2,1)}) %reduce-scatter.10.cloned.1.call-update) | async-done | bytes 393232
  425.6 2.0 reshape.169
  431.4 2.4 copy.76
  433.8 2.4 reshape.172
  436.2 19.6 %all-gather.8.cloned.1.call-done = bf16[16,32,1536]{2,1,0:T(8,128)(2,1)} async-done(((bf16[16,32,384]{2,1,0:T(8,128)(2,1)}), bf16[16,32,1536]{2,1,0:T(8,128)(2,1)}) %all-gather.8.cloned.1.call-update) | async-done | bytes 1572880 | tf_op jit(solution)/shard_map/all_gather | solution.py:144
  457.7 2.0 fusion.20
  459.7 8.9 %fusion.37 = bf16[16,32,1536]{2,1,0:T(8,128)(2,1)S(1)} fusion(bf16[1536,1536]{1,0:T(8,128)(2,1)} %param.31, bf16[1536,1536]{1,0:T(8,128)(2,1)} %param.30, bf16[16,32,1536]{2,1,0:T(8,128)(2,1)S(1)} %copy-done.3, f32[16,1536]{1,0:T(8,128)S(1)} %copy-done.14, f32[16,1536]{1,0:T(8,128)S(1)} %copy-done.13, f32[16,32]{1,0:T(8,128)S(1)} %add_rsqrt_fusion.4, ...), kind=kOutput, calls=%fused_computation.41 | convolution fusion | flops 4844421120 | bytes 12783616 | tf_op jit(solution)/shard_map/rsf,fd->rsd/dot_general | solution.py:152
  468.6 6.6 %copy.74 = bf16[16,32,1536]{1,0,2:T(8,128)(2,1)} copy(bf16[16,32,1536]{2,1,0:T(8,128)(2,1)S(1)} %fusion.37) | data formatting | bytes 3145728
  475.2 9.3 %reshape.170 = bf16[1536,512]{1,0:T(8,128)(2,1)} reshape(bf16[1536,16,32]{2,1,0:T(8,128)(2,1)} %bitcast.111) | data formatting | bytes 3145728
  484.6 2.3 reshape.173
  486.8 2.1 copy.77
  490.4 19.0 %reduce-scatter.12.cloned.1.call-done = bf16[384,512]{1,0:T(8,128)(2,1)} async-done(((bf16[1536,512]{1,0:T(8,128)(2,1)}), bf16[384,512]{1,0:T(8,128)(2,1)}) %reduce-scatter.12.cloned.1.call-update) | async-done | bytes 393232
  509.5 2.9 reshape.171
  512.3 2.6 copy.75
  514.9 2.0 add_convert_fusion
  (116 shorter events, 37.3 us)
Async XLA Ops:
  7.2 34.9 %copy-start = (bf16[1536,3,384]{2,0,1:T(8,128)(2,1)S(1)}, bf16[1536,3,384]{2,0,1:T(8,128)(2,1)}, u32[]{:S(2)}) copy-start(bf16[1536,3,384]{2,0,1:T(8,128)(2,1)} %param.22) | copy-start | bytes 10616836
  7.2 31.0 %all-gather.4.cloned.1.call-start = ((), (), s32[]{:S(2)}) async-start(), calls=%async_computation.3 | async-start | bytes 1966080 | tf_op jit(solution)/shard_map/all_gather | solution.py:73
  7.9 278.4 %all-gather.6.cloned.1.call-start = ((), (), s32[]{:S(2)}) async-start(), calls=%async_computation.4 | async-start | bytes 30007296 | tf_op jit(solution)/shard_map/all_gather | solution.py:97
  18.9 0.7 copy-start.8
  19.6 13.5 %copy-start.17 = (s32[16]{0:T(128)S(1)}, s32[16]{0:T(128)}, u32[]{:S(2)}) copy-start(s32[16]{0:T(128)} %param.18) | copy-start | bytes 196
  22.5 0.8 copy-start.9
  34.5 0.8 copy-start.5
  38.2 3.8 copy-start.2
  38.2 3.8 copy-start.15
  38.2 3.8 copy-start.16
  44.5 1.5 copy-start.4
  48.2 3.2 copy-start.11
  49.5 1.9 copy-start.7
  49.6 1.9 copy-start.12
  51.4 1.6 copy-start.10
  51.4 2.1 copy-start.20
  51.4 2.3 copy-start.18
  52.7 372.9 %reduce-scatter.10.cloned.1.call-start = ((), (), s32[]{:S(2)}) async-start(), calls=%async_computation.6 | async-start | bytes 1966080
  53.5 1.6 copy-start.19
  403.1 25.7 %copy-start.6 = (bf16[16,32,384]{2,1,0:T(8,128)(2,1)S(1)}, bf16[16,32,384]{2,1,0:T(8,128)(2,1)}, u32[]{:S(2)}) copy-start(bf16[16,32,384]{2,1,0:T(8,128)(2,1)} %param.16) | copy-start | bytes 1179652
  403.2 52.7 %all-gather.8.cloned.1.call-start = ((), (), s32[]{:S(2)}) async-start(), calls=%async_computation.5 | async-start | bytes 1966080 | tf_op jit(solution)/shard_map/all_gather | solution.py:144
  429.7 54.8 %reduce-scatter.14.cloned.1.call-start = ((), (), s32[]{:S(2)}) async-start(), calls=%async_computation.8 | async-start | bytes 491520
  433.8 25.9 %copy-start.13 = (f32[16,1536]{1,0:T(8,128)S(1)}, f32[16,1536]{1,0:T(8,128)}, u32[]{:S(2)}) copy-start(f32[16,1536]{1,0:T(8,128)} %get-tuple-element.8) | copy-start | bytes 294916
  433.8 25.9 %copy-start.14 = (f32[16,1536]{1,0:T(8,128)S(1)}, f32[16,1536]{1,0:T(8,128)}, u32[]{:S(2)}) copy-start(f32[16,1536]{1,0:T(8,128)} %get-tuple-element.9) | copy-start | bytes 294916
  436.2 73.3 %reduce-scatter.12.cloned.1.call-start = ((), (), s32[]{:S(2)}) async-start(), calls=%async_computation.7 | async-start | bytes 1966080
  455.9 3.8 copy-start.3
  484.5 32.4 %copy-start.1 = (bf16[1536,3,384]{2,0,1:T(8,128)(2,1)S(1)}, bf16[1536,3,384]{2,0,1:T(8,128)(2,1)}, u32[]{:S(2)}) copy-start(bf16[1536,3,384]{2,0,1:T(8,128)(2,1)} %param.22) | copy-start | bytes 10616836
Sparse Core Ops, SparseCore 0:
  9.7 28.4 all-gather.3
  52.9 233.4 all-gather.5
  403.3 22.3 reduce-scatter.9
  429.8 25.9 all-gather.7
  458.1 18.7 reduce-scatter.13
  484.6 24.7 reduce-scatter.11
where the time goes:
time: 526 us; the launch traced here: 524 us
  waiting for transfers between devices  293 us (56%)
  local copies, waits for them, and re-layouts  130 us (25%)
  matrix products  45.9 us (9%)
  other arithmetic  32 us (6%)
  between operations  14.6 us (3%)
  blocking collectives  7.62 us (1%)
    all_gather x1, waiting for transfers between devices, per_device(): shard_piece = lax.all_gather(key_value, 'tile', axis=1, tiled=True)  231 us
    unnamed x56, local copies, waits for them, and re-layouts  92.3 us
    unnamed x9, waiting for transfers between devices  40.6 us
    slice x1, local copies, waits for them, and re-layouts, per_device(): shard_piece[:, :, 0].reshape(requests, piece_rows, head_count, HEAD_DIM)  21.9 us
    all_gather x1, waiting for transfers between devices, per_device(): middle_whole = lax.all_gather(image_mid, 'blk', axis=2, tiled=True)  19.6 us
    dot_general x1, matrix products, per_device(): jnp.einsum('rhqk,rkhe->rhqe', weights.astype(jnp.bfloat16), piece_values,...  13.1 us
    dot_general x1, matrix products, per_device(): jnp.einsum('rqhe,rkhe->rhqk', joint_q, piece_keys, preferred_element_type...  12.2 us
  transfers between devices with their start and end apart: 6, of which 5 were waited for; matrix products, arithmetic and copies ran while one was open for 12% of the time, Pallas kernels for 0%

commit v1 on v0

--- a/solution.py
+++ b/solution.py
@@ -94,7 +94,9 @@
         ],
         axis=2,
     )
-    shard_piece = lax.all_gather(key_value, "tile", axis=1, tiled=True)
+    shard_piece = jnp.concatenate(
+        lax.all_to_all(jnp.stack([key_value] * lax.axis_size("tile")), "tile", 0, 0), axis=1
+    )
     running_max = jnp.full((requests, head_count, joint_rows, 1), masked_score, jnp.float32)
     piece_rows = shard_piece.shape[1]
     position = jnp.arange(piece_rows, dtype=jnp.int32)

time: 526 us -> 866 us (1.65)
  waiting for transfers between devices: 293 us -> 615 us
  starting transfers between devices: 0.64 us -> 9.98 us
  local copies, waits for them, and re-layouts: 130 us -> 139 us
    all_to_all x0 -> x1, waiting for transfers between devices: none -> 463 us  [per_device(): lax.all_to_all(jnp.stack([key_value] * lax.axis_size('tile')), 'tile', 0, 0)]
    all_gather x1 -> x0, waiting for transfers between devices: 231 us -> none  [per_device(): shard_piece = lax.all_gather(key_value, 'tile', axis=1, tiled=True)]
    unnamed x9 -> x8, waiting for transfers between devices: 40.6 us -> 131 us
    unnamed x56 -> x54, local copies, waits for them, and re-layouts: 92.3 us -> 51.9 us
    slice x1 -> x2, local copies, waits for them, and re-layouts: 21.9 us -> 42.1 us  [per_device(): shard_piece[:, :, 0].reshape(requests, piece_rows, head_count, HEAD_DIM)]
    slice x0 -> x1, local copies, waits for them, and re-layouts: none -> 20.2 us  [per_device(): shard_piece[:, :, 1].reshape(requests, piece_rows, head_count, HEAD_DIM)]
    another operation x0 -> x1, local copies, waits for them, and re-layouts: none -> 9.8 us  [per_device(): jnp.stack([key_value] * lax.axis_size('tile'))]
    all_to_all x0 -> x1, starting transfers between devices: none -> 9.37 us  [per_device(): lax.all_to_all(jnp.stack([key_value] * lax.axis_size('tile')), 'tile', 0, 0)]
  transfers between devices with their start and end apart: 6 -> 6, of which waited for: 5 -> 5; matrix products, arithmetic and copies ran while one was open for 12% -> 7% of each run, Pallas kernels for 0% -> 0%
where the time goes in v1:
time: 866 us; the launch traced here: 864 us
  waiting for transfers between devices  615 us (71%)
  local copies, waits for them, and re-layouts  139 us (16%)
  matrix products  45.8 us (5%)
  other arithmetic  32 us (4%)
  between operations  14.3 us (2%)
  starting transfers between devices  9.98 us (1%)
    all_to_all x1, waiting for transfers between devices, per_device(): lax.all_to_all(jnp.stack([key_value] * lax.axis_size('tile')), 'tile', 0, 0)  463 us
    unnamed x8, waiting for transfers between devices  131 us
    unnamed x54, local copies, waits for them, and re-layouts  51.9 us
    slice x2, local copies, waits for them, and re-layouts, per_device(): shard_piece[:, :, 0].reshape(requests, piece_rows, head_count, HEAD_DIM)  42.1 us
    slice x1, local copies, waits for them, and re-layouts, per_device(): shard_piece[:, :, 1].reshape(requests, piece_rows, head_count, HEAD_DIM)  20.2 us
    all_gather x1, waiting for transfers between devices, per_device(): middle_whole = lax.all_gather(image_mid, 'blk', axis=2, tiled=True)  19.6 us
  transfers between devices with their start and end apart: 6, of which 5 were waited for; matrix products, arithmetic and copies ran while one was open for 7% of the time, Pallas kernels for 0%

profile of v1, /device:TPU:1, one launch (start us, length us, event | category | flops | bytes accessed | tf_op | source)
XLA Modules:
  0.0 863.9 jit_solution(13629913809127929448)
XLA Ops:
  9.7 7.6 all_gather.10
  19.7 2.8 fusion.16
  36.1 2.2 all-gather.3.cloned.1.call-done
  40.1 2.0 fusion.24
  42.1 2.4 fusion.18
  51.7 9.8 %stack.5 = bf16[32,16,37,2,384]{4,1,3,2,0:T(8,128)(2,1)} broadcast(bf16[16,37,2,384]{3,0,2,1:T(8,128)(2,1)S(1)} %copy.65), dimensions={1,2,3,4} | broadcast | bytes 30007296 | tf_op jit(solution)/shard_map/stack | solution.py:98
  61.5 9.4 %all-to-all-start = ((bf16[32,16,37,2,384]{4,1,3,2,0:T(8,128)(2,1)}), bf16[32,16,37,2,384]{4,1,3,2,0:T(8,128)(2,1)}, u32[]{:S(2)}, u32[]{:S(2)}) async-start(bf16[32,16,37,2,384]{4,1,3,2,0:T(8,128)(2,1)} %stack.5), calls=%async_computation | async-start | bytes 58195968 | tf_op jit(solution)/shard_map/all_to_all | solution.py:98
  73.8 463.1 %all-to-all-done = bf16[32,16,37,2,384]{4,1,3,2,0:T(8,128)(2,1)} async-done(((bf16[32,16,37,2,384]{4,1,3,2,0:T(8,128)(2,1)}), bf16[32,16,37,2,384]{4,1,3,2,0:T(8,128)(2,1)}, u32[]{:S(2)}, u32[]{:S(2)}) %all-to-all-start) | async-done | bytes 29098016 | tf_op jit(solution)/shard_map/all_to_all | solution.py:98
  536.9 21.9 %fusion.114 = (bf16[16,1184,1,384]{3,0,2,1:T(8,128)(2,1)}, bf16[16,1184,1,384]{3,0,2,1:T(8,128)(2,1)}) fusion(bf16[16,1184,2,384]{3,0,2,1:T(8,128)(2,1)} %bitcast.15), kind=kLoop, calls=%fused_computation.149 | loop fusion | bytes 58195968 | tf_op jit(solution)/shard_map/slice | solution.py:106
  558.8 20.2 %copy.66 = bf16[16,1184,1,384]{1,3,0,2:T(8,128)(2,1)} copy(bf16[16,1184,1,384]{3,0,2,1:T(8,128)(2,1)} %get-tuple-element.2) | data formatting | bytes 29097984 | tf_op jit(solution)/shard_map/slice | solution.py:106
  579.0 12.2 %select_reduce_fusion = (f32[16,6,37]{2,1,0:T(8,128)S(1)}, f32[16,6,37,1184]{3,2,1,0:T(8,128)}) fusion(pred[16,1184]{1,0:T(8,128)(4,1)S(1)} %compare_or_fusion, bf16[16,1184,6,64]{1,3,2,0:T(8,128)(2,1)} %bitcast.112, bf16[16,5,6,64]{3,1,2,0:T(8,128)(2,1)S(1)} %fusion.79, bf16[16,32,6,64]{3,1,2,0:T(8,128)(2,1)S(1)} %fusion.50), kind=kOutput, calls=%fused_computation.1 | convolution fusion | flops 551835136 | bytes 31859072 | tf_op jit(solution)/shard_map/rqhe,rkhe->rhqk/dot_general | solution.py:109
  591.2 20.2 %copy.67 = bf16[16,1184,1,384]{1,3,0,2:T(8,128)(2,1)} copy(bf16[16,1184,1,384]{3,0,2,1:T(8,128)(2,1)} %get-tuple-element.3) | data formatting | bytes 29097984 | tf_op jit(solution)/shard_map/slice | solution.py:107
  611.4 9.8 %fusion = f32[16,6,37]{2,1,0:T(8,128)S(1)} fusion(f32[16,6,37,1184]{3,2,1,0:T(8,128)} %get-tuple-element.17, f32[16,6,37]{2,1,0:T(8,128)S(1)} %broadcast_maximum_fusion, pred[16,1184]{1,0:T(8,128)(4,1)S(1)} %compare_or_fusion), kind=kLoop, calls=%fused_computation.2 | loop fusion | flops 16818720 | bytes 16869632 | tf_op jit(solution)/shard_map/reduce_sum | solution.py:117
  621.2 13.1 %fusion.43 = bf16[16,37,6,64]{3,1,2,0:T(8,128)(2,1)S(1)} fusion(bf16[16,1184,6,64]{1,3,2,0:T(8,128)(2,1)} %bitcast.115, f32[16,6,37,1184]{3,2,1,0:T(8,128)} %get-tuple-element.17, f32[16,6,37]{2,1,0:T(8,128)S(1)} %broadcast_maximum_fusion, pred[16,1184]{1,0:T(8,128)(4,1)S(1)} %compare_or_fusion, f32[16,37,6]{1,2,0:T(8,128)S(1)} %bitcast.120), kind=kOutput, calls=%fused_computation.47 | convolution fusion | flops 555589632 | bytes 31873280 | tf_op jit(solution)/shard_map/rhqk,rkhe->rhqe/dot_general | solution.py:118
  635.4 2.3 convolution_convert_fusion
  637.7 6.6 copy.72
  644.3 9.3 %reshape.178 = bf16[1536,512]{1,0:T(8,128)(2,1)} reshape(bf16[1536,16,32]{2,1,0:T(8,128)(2,1)} %bitcast.113) | data formatting | bytes 3145728
  655.3 110.8 %reduce-scatter.10.cloned.1.call-done = bf16[384,512]{1,0:T(8,128)(2,1)} async-done(((bf16[1536,512]{1,0:T(8,128)(2,1)}), bf16[384,512]{1,0:T(8,128)(2,1)}) %reduce-scatter.10.cloned.1.call-update) | async-done | bytes 393232
  766.1 2.0 reshape.179
  771.8 2.4 copy.76
  774.2 2.4 reshape.182
  776.7 19.6 %all-gather.5.cloned.1.call-done = bf16[16,32,1536]{2,1,0:T(8,128)(2,1)} async-done(((bf16[16,32,384]{2,1,0:T(8,128)(2,1)}), bf16[16,32,1536]{2,1,0:T(8,128)(2,1)}) %all-gather.5.cloned.1.call-update) | async-done | bytes 1572880 | tf_op jit(solution)/shard_map/all_gather | solution.py:146
  798.1 2.0 fusion.20
  800.1 8.9 %fusion.37 = bf16[16,32,1536]{2,1,0:T(8,128)(2,1)S(1)} fusion(bf16[1536,1536]{1,0:T(8,128)(2,1)} %param.31, bf16[1536,1536]{1,0:T(8,128)(2,1)} %param.30, bf16[16,32,1536]{2,1,0:T(8,128)(2,1)S(1)} %copy-done.3, f32[16,1536]{1,0:T(8,128)S(1)} %copy-done.14, f32[16,1536]{1,0:T(8,128)S(1)} %copy-done.13, f32[16,32]{1,0:T(8,128)S(1)} %add_rsqrt_fusion.4, ...), kind=kOutput, calls=%fused_computation.41 | convolution fusion | flops 4844421120 | bytes 12783616 | tf_op jit(solution)/shard_map/rsf,fd->rsd/dot_general | solution.py:154
  809.0 6.6 copy.74
  815.6 9.3 %reshape.180 = bf16[1536,512]{1,0:T(8,128)(2,1)} reshape(bf16[1536,16,32]{2,1,0:T(8,128)(2,1)} %bitcast.114) | data formatting | bytes 3145728
  825.0 2.3 reshape.183
  827.3 2.1 copy.77
  830.8 19.0 %reduce-scatter.12.cloned.1.call-done = bf16[384,512]{1,0:T(8,128)(2,1)} async-done(((bf16[1536,512]{1,0:T(8,128)(2,1)}), bf16[384,512]{1,0:T(8,128)(2,1)}) %reduce-scatter.12.cloned.1.call-update) | async-done | bytes 393232
  849.8 2.9 reshape.181
  852.7 2.6 copy.75
  855.3 2.0 add_convert_fusion
  (116 shorter events, 40.0 us)
Async XLA Ops:
  7.2 34.9 %copy-start = (bf16[1536,3,384]{2,0,1:T(8,128)(2,1)S(1)}, bf16[1536,3,384]{2,0,1:T(8,128)(2,1)}, u32[]{:S(2)}) copy-start(bf16[1536,3,384]{2,0,1:T(8,128)(2,1)} %param.22) | copy-start | bytes 10616836
  7.2 31.0 %all-gather.3.cloned.1.call-start = ((), (), s32[]{:S(2)}) async-start(), calls=%async_computation.4 | async-start | bytes 1966080 | tf_op jit(solution)/shard_map/all_gather | solution.py:73
  18.9 0.8 copy-start.8
  19.6 13.5 %copy-start.17 = (s32[16]{0:T(128)S(1)}, s32[16]{0:T(128)}, u32[]{:S(2)}) copy-start(s32[16]{0:T(128)} %param.18) | copy-start | bytes 196
  22.5 0.8 copy-start.9
  34.5 0.8 copy-start.5
  38.2 3.8 copy-start.2
  38.2 3.8 copy-start.15
  38.2 3.8 copy-start.16
  44.5 1.5 copy-start.4
  48.1 3.2 copy-start.11
  48.2 3.2 copy-start.12
  49.6 1.8 copy-start.7
  61.5 9.6 %copy-start.10 = (f32[16,5,1,384]{3,0,2,1:T(8,128)S(1)}, f32[16,5,1,384]{3,0,2,1:T(8,128)}, u32[]{:S(2)}) copy-start(f32[16,5,1,384]{3,0,2,1:T(8,128)} %get-tuple-element.12) | copy-start | bytes 368644
  61.5 10.2 %copy-start.20 = (f32[64]{0:T(128)S(1)}, f32[64]{0:T(128)}, u32[]{:S(2)}) copy-start(f32[64]{0:T(128)} %param.28) | copy-start | bytes 772
  61.5 10.4 %copy-start.18 = (s32[16]{0:T(128)S(1)}, s32[16]{0:T(128)}, u32[]{:S(2)}) copy-start(s32[16]{0:T(128)} %param.19) | copy-start | bytes 196
  61.5 475.4 %all-to-all-start = ((bf16[32,16,37,2,384]{4,1,3,2,0:T(8,128)(2,1)}), bf16[32,16,37,2,384]{4,1,3,2,0:T(8,128)(2,1)}, u32[]{:S(2)}, u32[]{:S(2)}) async-start(bf16[32,16,37,2,384]{4,1,3,2,0:T(8,128)(2,1)} %stack.5), calls=%async_computation | async-start | bytes 58195968 | tf_op jit(solution)/shard_map/all_to_all | solution.py:98
  70.9 695.2 %reduce-scatter.10.cloned.1.call-start = ((), (), s32[]{:S(2)}) async-start(), calls=%async_computation.6 | async-start | bytes 1966080
  71.7 1.6 copy-start.19
  653.6 115.7 %copy-start.6 = (bf16[16,32,384]{2,1,0:T(8,128)(2,1)S(1)}, bf16[16,32,384]{2,1,0:T(8,128)(2,1)}, u32[]{:S(2)}) copy-start(bf16[16,32,384]{2,1,0:T(8,128)(2,1)} %param.16) | copy-start | bytes 1179652
  653.6 142.7 %all-gather.5.cloned.1.call-start = ((), (), s32[]{:S(2)}) async-start(), calls=%async_computation.5 | async-start | bytes 1966080 | tf_op jit(solution)/shard_map/all_gather | solution.py:146
  770.2 54.8 %reduce-scatter.14.cloned.1.call-start = ((), (), s32[]{:S(2)}) async-start(), calls=%async_computation.8 | async-start | bytes 491520
  774.2 25.8 %copy-start.13 = (f32[16,1536]{1,0:T(8,128)S(1)}, f32[16,1536]{1,0:T(8,128)}, u32[]{:S(2)}) copy-start(f32[16,1536]{1,0:T(8,128)} %get-tuple-element.8) | copy-start | bytes 294916
  774.2 25.8 %copy-start.14 = (f32[16,1536]{1,0:T(8,128)S(1)}, f32[16,1536]{1,0:T(8,128)}, u32[]{:S(2)}) copy-start(f32[16,1536]{1,0:T(8,128)} %get-tuple-element.9) | copy-start | bytes 294916
  776.6 73.2 %reduce-scatter.12.cloned.1.call-start = ((), (), s32[]{:S(2)}) async-start(), calls=%async_computation.7 | async-start | bytes 1966080
  796.3 3.8 copy-start.3
  825.0 32.4 %copy-start.1 = (bf16[1536,3,384]{2,0,1:T(8,128)(2,1)S(1)}, bf16[1536,3,384]{2,0,1:T(8,128)(2,1)}, u32[]{:S(2)}) copy-start(bf16[1536,3,384]{2,0,1:T(8,128)(2,1)} %param.22) | copy-start | bytes 10616836
Sparse Core Ops, SparseCore 0:
  9.7 28.4 all-gather.2
  653.7 112.3 reduce-scatter.9
  770.3 25.9 all-gather.4
  798.5 18.7 reduce-scatter.13
  825.1 24.7 reduce-scatter.11
